TPU v7x, 32 devices: a whole 2x2x4 slice. The times are simulated.
32 devices in a mesh: dp: 8 (over y, x, core), tensor: 4 (over z).
Axes of the slice: x: 2, y: 2, z: 4, core: 2. Of those that a mesh axis runs over, the one named last changes fastest.
Arguments:
- inputs: bfloat16 [8192, 1536], P(('dp', 'tensor')), may hold values from -12 to 12
- norm1_gain: float32 [1536], replicated, may hold values from 0.5 to 1.5
- w_in_x: bfloat16 [1536, 2048], P('dp', 'tensor'), may hold values from -0.15625 to 0.15625
- w_in_y: bfloat16 [1536, 2048], P('dp', 'tensor'), may hold values from -0.15625 to 0.15625
- conv_w: float32 [4, 2048], P(None, 'tensor'), may hold values from -3 to 3
- conv_b: float32 [2048], P('tensor'), may hold values from -1.8 to 1.8
- gates: bfloat16 [2, 16, 128, 128], P(None, 'tensor', 'dp'), may hold values from -0.5 to 0.5
- gate_bias: float32 [2, 2048], P(None, 'tensor'), may hold values from -1 to 1
- decay_param: float32 [2048], P('tensor'), may hold values from -7 to -1
- w_out: bfloat16 [1536, 2048], P('dp', 'tensor'), may hold values from -0.375 to 0.375
- norm2_gain: float32 [1536], replicated, may hold values from 0.5 to 1.5
- w_gate: bfloat16 [1536, 4608], P('dp', 'tensor'), may hold values from -0.15625 to 0.15625
- w_up: bfloat16 [1536, 4608], P('dp', 'tensor'), may hold values from -0.15625 to 0.15625
- w_down: bfloat16 [1536, 4608], P('dp', 'tensor'), may hold values from -0.125 to 0.125
- cotangent: bfloat16 [8192, 1536], P(('dp', 'tensor')), may hold values from -6 to 6
Outputs:
- output: bfloat16 [8192, 1536], P(('dp', 'tensor'))
- grad_inputs: bfloat16 [8192, 1536], P(('dp', 'tensor'))
- grad_norm1_gain: float32 [1536], replicated
- grad_w_in_x: float32 [1536, 2048], P('dp', 'tensor')
- grad_w_in_y: float32 [1536, 2048], P('dp', 'tensor')
- grad_conv_w: float32 [4, 2048], replicated
- grad_conv_b: float32 [2048], replicated
- grad_gates: float32 [2, 16, 128, 128], P(None, 'tensor', 'dp')
- grad_gate_bias: float32 [2, 2048], replicated
- grad_decay_param: float32 [2048], replicated
- grad_w_out: float32 [1536, 2048], P('dp', 'tensor')
- grad_norm2_gain: float32 [1536], replicated
- grad_w_gate: float32 [1536, 4608], P('dp', 'tensor')
- grad_w_up: float32 [1536, 4608], P('dp', 'tensor')
- grad_w_down: float32 [1536, 4608], P('dp', 'tensor')
- stream_rms: float32 [4], replicated
All inputs are finite; a program needn't handle non-finite values.
Results may differ from a plain program's by a relative error of at most 0.0085.
Values may be sent and summed in bfloat16 or wider, within the bound.
A program may use at most 192 MiB of HBM per device.

v0:
```python
import jax
import jax.numpy as jnp
from jax import lax
from jax.sharding import PartitionSpec as P

CONV = 4
SEQ_LEN = 1024
epsilon = 1e-06


def gelu_tanh(value):
    return jax.nn.gelu(value, approximate=True)


def combine(earlier, later):
    return (earlier[0] * later[0], later[0] * earlier[1] + later[1])


def norm_back(value, scale, gain, grad):
    scaled = gain * grad
    return scale * scaled - value * scale * scale * scale * jnp.mean(
        scaled * value, axis=1, keepdims=True
    )


def row_product(left, right):
    return lax.dot_general(
        left, right, (((0,), (0,)), ((), ())), preferred_element_type=jnp.float32
    )


def back_product(left, right):
    return lax.dot_general(
        left, right, (((1,), (1,)), ((), ())), preferred_element_type=jnp.float32
    )


def local(
    inputs,
    norm1_gain,
    w_in_x,
    w_in_y,
    conv_w,
    conv_b,
    gates,
    gate_bias,
    decay_param,
    w_out,
    norm2_gain,
    w_gate,
    w_up,
    w_down,
    cotangent,
):
    row_count = inputs.shape[0]
    model_width = inputs.shape[1]
    tensor_count = lax.axis_size("tensor")
    group_rows = row_count * tensor_count
    seq_count = group_rows // SEQ_LEN
    rec_x, rec_y, rec_o, gate_mats = (
        lax.all_gather(w_in_x, "dp", axis=0, tiled=True),
        lax.all_gather(w_in_y, "dp", axis=0, tiled=True),
        lax.all_gather(w_out, "dp", axis=0, tiled=True),
        lax.all_gather(gates, "dp", axis=2, tiled=True),
    )
    channels = rec_x.shape[1]
    blocks_here = gate_mats.shape[1]
    block_width = gate_mats.shape[3]
    residual = inputs.astype(jnp.float32)
    scale_one = lax.rsqrt(jnp.mean(residual * residual, axis=1, keepdims=True) + epsilon)
    n_one = (residual * scale_one * norm1_gain).astype(jnp.bfloat16)
    full_one = lax.all_gather(n_one, "tensor", axis=0, tiled=True)
    x_branch = jnp.dot(full_one, rec_x, preferred_element_type=jnp.float32)
    y_pre = jnp.dot(full_one, rec_y, preferred_element_type=jnp.float32)
    seq_x = x_branch.reshape(seq_count, SEQ_LEN, channels)
    padded = jnp.pad(seq_x, ((0, 0), (CONV - 1, 0), (0, 0)))
    conv_sum = conv_b + jnp.zeros_like(seq_x)
    for k in range(CONV):
        conv_sum = conv_sum + conv_w[k] * padded[:, CONV - 1 - k : CONV - 1 - k + SEQ_LEN]
    conv_low = conv_sum.reshape(group_rows, channels).astype(jnp.bfloat16)
    conv_value = conv_low.astype(jnp.float32)
    blocked = conv_low.reshape(group_rows, blocks_here, block_width)
    z_input = (
        jnp.einsum(
            "gbi,bij->gbj", blocked, gate_mats[0], preferred_element_type=jnp.float32
        ).reshape(group_rows, channels)
        + gate_bias[0]
    )
    z_decay = (
        jnp.einsum(
            "gbi,bij->gbj", blocked, gate_mats[1], preferred_element_type=jnp.float32
        ).reshape(group_rows, channels)
        + gate_bias[1]
    )
    seq_start = (jnp.arange(group_rows) % SEQ_LEN == 0)[:, None]

    def coefficients(input_pre, decay_pre, conv_part, decay_raw):
        log_decay = -8.0 * jax.nn.sigmoid(decay_pre) * jax.nn.softplus(decay_raw)
        mult = jnp.where(seq_start, 1.0, jnp.sqrt(-jnp.expm1(2.0 * log_decay)))
        return (jnp.exp(log_decay), mult * jax.nn.sigmoid(input_pre) * conv_part)

    (decays, inflow), pull_coeff = jax.vjp(coefficients, z_input, z_decay, conv_value, decay_param)
    seq_decay = decays.reshape(seq_count, SEQ_LEN, channels)
    _, seq_states = lax.associative_scan(
        combine, (seq_decay, inflow.reshape(seq_count, SEQ_LEN, channels)), axis=1
    )
    states = seq_states.reshape(group_rows, channels)
    y_gate = gelu_tanh(y_pre)
    mixed_out = (states * y_gate).astype(jnp.bfloat16)
    branch = lax.psum_scatter(
        back_product(mixed_out, rec_o), "tensor", scatter_dimension=0, tiled=True
    )
    stream = residual + branch
    mlp_g, mlp_u, mlp_d = (
        lax.all_gather(w_gate, "dp", axis=0, tiled=True),
        lax.all_gather(w_up, "dp", axis=0, tiled=True),
        lax.all_gather(w_down, "dp", axis=0, tiled=True),
    )
    scale_two = lax.rsqrt(jnp.mean(stream * stream, axis=1, keepdims=True) + epsilon)
    n_two = (stream * scale_two * norm2_gain).astype(jnp.bfloat16)
    full_two = lax.all_gather(n_two, "tensor", axis=0, tiled=True)
    gate_pre = jnp.dot(full_two, mlp_g, preferred_element_type=jnp.float32)
    up_pre = jnp.dot(full_two, mlp_u, preferred_element_type=jnp.float32)
    hidden = (gelu_tanh(gate_pre) * up_pre).astype(jnp.bfloat16)
    ffn_out = lax.psum_scatter(
        back_product(hidden, mlp_d), "tensor", scatter_dimension=0, tiled=True
    )
    result = stream + ffn_out
    output = result.astype(jnp.bfloat16)
    squares = jnp.stack(
        [
            jnp.sum(stream * stream),
            jnp.sum(branch * branch),
            jnp.sum(ffn_out * ffn_out),
            jnp.sum(result * result),
        ]
    )
    upstream = cotangent.astype(jnp.float32)
    full_cot = lax.all_gather(cotangent, "tensor", axis=0, tiled=True)
    d_hidden = jnp.dot(full_cot, mlp_d, preferred_element_type=jnp.float32)
    grad_down = row_product(full_cot, hidden)
    _, pull_mlp = jax.vjp(
        lambda gate_value, up_value: gelu_tanh(gate_value) * up_value, gate_pre, up_pre
    )
    d_gate, d_up = pull_mlp(d_hidden)
    d_gate_low = d_gate.astype(jnp.bfloat16)
    d_up_low = d_up.astype(jnp.bfloat16)
    grad_gate_w = row_product(full_two, d_gate_low)
    grad_up_w = row_product(full_two, d_up_low)
    d_two = lax.psum_scatter(
        back_product(d_gate_low, mlp_g) + back_product(d_up_low, mlp_u),
        "tensor",
        scatter_dimension=0,
        tiled=True,
    )
    grad_gain_two = jnp.sum(d_two * stream * scale_two, axis=0)
    d_stream = upstream + norm_back(stream, scale_two, norm2_gain, d_two)
    mlp_summed = (grad_gate_w, grad_up_w, grad_down)
    full_branch = lax.all_gather(d_stream.astype(jnp.bfloat16), "tensor", axis=0, tiled=True)
    d_mixed = jnp.dot(full_branch, rec_o, preferred_element_type=jnp.float32)
    grad_out_w = row_product(full_branch, mixed_out)
    d_states = d_mixed * y_gate
    _, pull_gelu = jax.vjp(gelu_tanh, y_pre)
    d_y_low = pull_gelu(d_mixed * states)[0].astype(jnp.bfloat16)
    next_decay = jnp.concatenate([seq_decay[:, 1:], jnp.zeros_like(seq_decay[:, :1])], axis=1)
    _, carried = lax.associative_scan(
        combine, (next_decay, d_states.reshape(seq_count, SEQ_LEN, channels)), reverse=True, axis=1
    )
    prev_states = jnp.concatenate([jnp.zeros_like(seq_states[:, :1]), seq_states[:, :-1]], axis=1)
    d_decays = (carried * prev_states).reshape(group_rows, channels)
    d_input_pre, d_decay_pre, d_conv_direct, grad_decay = pull_coeff(
        (d_decays, carried.reshape(group_rows, channels))
    )
    d_input_low = d_input_pre.astype(jnp.bfloat16)
    d_decay_low = d_decay_pre.astype(jnp.bfloat16)
    grad_bias = jnp.stack(
        [
            jnp.sum(d_input_low, axis=0, dtype=jnp.float32),
            jnp.sum(d_decay_low, axis=0, dtype=jnp.float32),
        ]
    )
    input_blocks = d_input_low.reshape(group_rows, blocks_here, block_width)
    decay_blocks = d_decay_low.reshape(group_rows, blocks_here, block_width)
    grad_gate_mats = jnp.stack(
        [
            jnp.einsum("gbi,gbj->bij", blocked, input_blocks, preferred_element_type=jnp.float32),
            jnp.einsum("gbi,gbj->bij", blocked, decay_blocks, preferred_element_type=jnp.float32),
        ]
    )
    d_conv = d_conv_direct + jnp.einsum(
        "gbj,bij->gbi", input_blocks, gate_mats[0], preferred_element_type=jnp.float32
    ).reshape(group_rows, channels)
    d_conv = d_conv + jnp.einsum(
        "gbj,bij->gbi", decay_blocks, gate_mats[1], preferred_element_type=jnp.float32
    ).reshape(group_rows, channels)
    seq_dconv = d_conv.reshape(seq_count, SEQ_LEN, channels)
    grad_conv_b = jnp.sum(seq_dconv, axis=(0, 1))
    padded_back = jnp.pad(seq_dconv, ((0, 0), (0, CONV - 1), (0, 0)))
    tap_grads = []
    d_x_seq = jnp.zeros_like(seq_dconv)
    for k in range(CONV):
        tap_grads.append(
            jnp.sum(seq_dconv * padded[:, CONV - 1 - k : CONV - 1 - k + SEQ_LEN], axis=(0, 1))
        )
        d_x_seq = d_x_seq + conv_w[k] * padded_back[:, k : k + SEQ_LEN]
    grad_conv_w = jnp.stack(tap_grads)
    d_x_low = d_x_seq.reshape(group_rows, channels).astype(jnp.bfloat16)
    grad_in_x_w = row_product(full_one, d_x_low)
    grad_in_y_w = row_product(full_one, d_y_low)
    d_one = lax.psum_scatter(
        back_product(d_x_low, rec_x) + back_product(d_y_low, rec_y),
        "tensor",
        scatter_dimension=0,
        tiled=True,
    )
    grad_gain_one = jnp.sum(d_one * residual * scale_one, axis=0)
    grad_inputs = (d_stream + norm_back(residual, scale_one, norm1_gain, d_one)).astype(
        jnp.bfloat16
    )
    small_grads = jnp.concatenate(
        [grad_conv_w, grad_conv_b[None], grad_bias, grad_decay[None]], axis=0
    )
    spread_grads = lax.dynamic_update_slice(
        jnp.zeros((small_grads.shape[0], channels * tensor_count), jnp.float32),
        small_grads,
        (0, lax.axis_index("tensor") * channels),
    )
    gain_total, small_total, square_total = lax.psum(
        (jnp.stack([grad_gain_one, grad_gain_two]), spread_grads, squares), ("dp", "tensor")
    )
    stream_rms = jnp.sqrt(
        square_total / (row_count * lax.axis_size("dp") * tensor_count * model_width)
    )
    summed_all = (
        lax.psum_scatter(grad_in_x_w, "dp", scatter_dimension=0, tiled=True),
        lax.psum_scatter(grad_in_y_w, "dp", scatter_dimension=0, tiled=True),
        lax.psum_scatter(grad_out_w, "dp", scatter_dimension=0, tiled=True),
        lax.psum_scatter(grad_gate_mats, "dp", scatter_dimension=2, tiled=True),
        lax.psum_scatter(mlp_summed[0], "dp", scatter_dimension=0, tiled=True),
        lax.psum_scatter(mlp_summed[1], "dp", scatter_dimension=0, tiled=True),
        lax.psum_scatter(mlp_summed[2], "dp", scatter_dimension=0, tiled=True),
    )
    rec_summed = summed_all[:4]
    grad_gate_sum, grad_up_sum, grad_down_sum = (summed_all[4], summed_all[5], summed_all[6])
    return (
        output,
        grad_inputs,
        gain_total[0],
        rec_summed[0],
        rec_summed[1],
        small_total[0:CONV],
        small_total[CONV],
        rec_summed[3],
        small_total[CONV + 1 : CONV + 3],
        small_total[CONV + 3],
        rec_summed[2],
        gain_total[1],
        grad_gate_sum,
        grad_up_sum,
        grad_down_sum,
        stream_rms,
    )


def solution(mesh):
    return jax.shard_map(
        local,
        mesh=mesh,
        in_specs=(
            P(("dp", "tensor"), None),
            P(),
            P("dp", "tensor"),
            P("dp", "tensor"),
            P(None, "tensor"),
            P("tensor"),
            P(None, "tensor", "dp", None),
            P(None, "tensor"),
            P("tensor"),
            P("dp", "tensor"),
            P(),
            P("dp", "tensor"),
            P("dp", "tensor"),
            P("dp", "tensor"),
            P(("dp", "tensor"), None),
        ),
        out_specs=(
            P(("dp", "tensor"), None),
            P(("dp", "tensor"), None),
            P(),
            P("dp", "tensor"),
            P("dp", "tensor"),
            P(),
            P(),
            P(None, "tensor", "dp", None),
            P(),
            P(),
            P("dp", "tensor"),
            P(),
            P("dp", "tensor"),
            P("dp", "tensor"),
            P("dp", "tensor"),
            P(),
        ),
        check_vma=False,
    )
```

profile of v0, /device:TPU:0, one launch (start us, length us, event | category | flops | bytes accessed | tf_op | source)
XLA Modules:
  0.0 1922.4 jit_solution(16737749595569484958)
XLA Ops:
  13.7 11.2 all_gather.35
  26.0 12.7 all-gather.13.cloned.1.call-done
  38.7 65.7 %all-gather.11.cloned.1.call-done = bf16[1024,1536]{1,0:T(8,128)(2,1)} async-done(((bf16[256,1536]{1,0:T(8,128)(2,1)}), bf16[1024,1536]{1,0:T(8,128)(2,1)}) %all-gather.11.cloned.1.call-update) | async-done | bytes 3145744 | tf_op jit(solution)/shard_map/all_gather | solution.py:72
  342.5 108.9 %reduce-scatter.14.cloned.1.call-done = f32[256,1536]{1,0:T(8,128)} async-done(((f32[1024,1536]{1,0:T(8,128)}), f32[256,1536]{1,0:T(8,128)}) %reduce-scatter.14.cloned.1.call-update) | async-done | bytes 1572880 | tf_op jit(solution)/shard_map/reduce_scatter | solution.py:110
  458.6 29.1 %all-gather.21.cloned.1.call-done = bf16[1536,1152]{1,0:T(8,128)(2,1)} async-done(((bf16[192,1152]{1,0:T(8,128)(2,1)}), bf16[1536,1152]{1,0:T(8,128)(2,1)}) %all-gather.21.cloned.1.call-update) | async-done | bytes 3538960 | tf_op jit(solution)/shard_map/all_gather | solution.py:115
  487.7 65.7 %all-gather.19.cloned.1.call-done = bf16[1024,1536]{1,0:T(8,128)(2,1)} async-done(((bf16[256,1536]{1,0:T(8,128)(2,1)}), bf16[1024,1536]{1,0:T(8,128)(2,1)}) %all-gather.19.cloned.1.call-update) | async-done | bytes 3145744 | tf_op jit(solution)/shard_map/all_gather | solution.py:121
  562.7 25.2 %all-gather.23.cloned.1.call-done = bf16[1536,1152]{1,0:T(8,128)(2,1)} async-done(((bf16[192,1152]{1,0:T(8,128)(2,1)}), bf16[1536,1152]{1,0:T(8,128)(2,1)}) %all-gather.23.cloned.1.call-update) | async-done | bytes 3538960 | tf_op jit(solution)/shard_map/all_gather | solution.py:116
  597.3 55.7 %all-gather.27.cloned.1.call-done = bf16[1024,1536]{1,0:T(8,128)(2,1)} async-done(((bf16[256,1536]{1,0:T(8,128)(2,1)}), bf16[1024,1536]{1,0:T(8,128)(2,1)}) %all-gather.27.cloned.1.call-update) | async-done | bytes 3145744 | tf_op jit(solution)/shard_map/all_gather | solution.py:139
  653.0 34.4 %all-gather.25.cloned.1.call-done = bf16[1536,1152]{1,0:T(8,128)(2,1)} async-done(((bf16[192,1152]{1,0:T(8,128)(2,1)}), bf16[1536,1152]{1,0:T(8,128)(2,1)}) %all-gather.25.cloned.1.call-update) | async-done | bytes 3538960 | tf_op jit(solution)/shard_map/all_gather | solution.py:117
  687.4 13.0 multiply_convert_fusion
  720.8 101.2 %reduce-scatter.18.cloned.1.call-done = f32[256,1536]{1,0:T(8,128)} async-done(((f32[1024,1536]{1,0:T(8,128)}), f32[256,1536]{1,0:T(8,128)}) %reduce-scatter.18.cloned.1.call-update) | async-done | bytes 1572880 | tf_op jit(solution)/shard_map/reduce_scatter | solution.py:150
  822.0 113.4 %reduce-scatter.16.cloned.1.call-done = f32[256,1536]{1,0:T(8,128)} async-done(((f32[1024,1536]{1,0:T(8,128)}), f32[256,1536]{1,0:T(8,128)}) %reduce-scatter.16.cloned.1.call-update) | async-done | bytes 1572880 | tf_op jit(solution)/shard_map/reduce_scatter | solution.py:125
  1015.3 16.6 reverse.6
  1221.8 16.7 rev.8
  1362.0 40.5 %all-reduce.47.cloned.1.call-done = f32[8,2048]{1,0:T(8,128)} async-done(((f32[8,2048]{1,0:T(8,128)}), f32[8,2048]{1,0:T(8,128)}) %all-reduce.47.cloned.1.call-update) | async-done | bytes 65552 | tf_op jit(solution)/shard_map/psum | solution.py:228
  1407.0 109.3 %reduce-scatter.20.cloned.1.call-done = f32[256,1536]{1,0:T(8,128)} async-done(((f32[1024,1536]{1,0:T(8,128)}), f32[256,1536]{1,0:T(8,128)}) %reduce-scatter.20.cloned.1.call-update) | async-done | bytes 1572880 | tf_op jit(solution)/shard_map/reduce_scatter | solution.py:210
  1518.1 41.2 %all-reduce.44 = (f32[2,1536]{1,0:T(2,128)S(1)}, f32[4]{0:T(128)S(1)}) all-reduce(f32[2,1536]{1,0:T(2,128)S(1)} %pad_maximum_fusion.15, f32[4]{0:T(128)S(1)} %pad_maximum_fusion.20), channel_id=1, replica_groups=mesh['dp'=8,'tensor'=4] {'dp','tensor'}, use_global_device_ids=true, to_apply=%region_10.11 | all-reduce | flops 3076 | bytes 24608 | tf_op jit(solution)/shard_map/psum | solution.py:228
  1564.3 22.5 %reduce-scatter.30.cloned.1.call-done = f32[192,1152]{1,0:T(8,128)} async-done(((f32[1536,1152]{1,0:T(8,128)}), f32[192,1152]{1,0:T(8,128)}) %reduce-scatter.30.cloned.1.call-update) | async-done | bytes 884752 | tf_op jit(solution)/shard_map/reduce_scatter | solution.py:239
  1586.9 69.9 %reduce-scatter.32.cloned.1.call-done = f32[192,1152]{1,0:T(8,128)} async-done(((f32[1536,1152]{1,0:T(8,128)}), f32[192,1152]{1,0:T(8,128)}) %reduce-scatter.32.cloned.1.call-update) | async-done | bytes 884752 | tf_op jit(solution)/shard_map/reduce_scatter | solution.py:240
  1656.8 69.5 %reduce-scatter.34.cloned.1.call-done = f32[192,1152]{1,0:T(8,128)} async-done(((f32[1536,1152]{1,0:T(8,128)}), f32[192,1152]{1,0:T(8,128)}) %reduce-scatter.34.cloned.1.call-update) | async-done | bytes 884752
  1726.2 38.1 %reduce-scatter.26.cloned.1.call-done = f32[2,4,16,128]{3,2,1,0:T(8,128)} async-done(((f32[2,4,128,128]{3,2,1,0:T(8,128)}), f32[2,4,16,128]{3,2,1,0:T(8,128)}) %reduce-scatter.26.cloned.1.call-update) | async-done | bytes 65552 | tf_op jit(solution)/shard_map/reduce_scatter | solution.py:238
  1764.3 50.1 %reduce-scatter.22.cloned.1.call-done = f32[192,512]{1,0:T(8,128)} async-done(((f32[1536,512]{1,0:T(8,128)}), f32[192,512]{1,0:T(8,128)}) %reduce-scatter.22.cloned.1.call-update) | async-done | bytes 393232 | tf_op jit(solution)/shard_map/reduce_scatter | solution.py:235
  1814.4 50.6 %reduce-scatter.28.cloned.1.call-done = f32[192,512]{1,0:T(8,128)} async-done(((f32[1536,512]{1,0:T(8,128)}), f32[192,512]{1,0:T(8,128)}) %reduce-scatter.28.cloned.1.call-update) | async-done | bytes 393232 | tf_op jit(solution)/shard_map/reduce_scatter | solution.py:237
  1865.0 50.2 %reduce-scatter.24.cloned.1.call-done = f32[192,512]{1,0:T(8,128)} async-done(((f32[1536,512]{1,0:T(8,128)}), f32[192,512]{1,0:T(8,128)}) %reduce-scatter.24.cloned.1.call-update) | async-done | bytes 393232 | tf_op jit(solution)/shard_map/reduce_scatter | solution.py:236
  (547 shorter events, 694.6 us)
Async XLA Ops:
  7.2 31.5 %all-gather.13.cloned.1.call-start = ((), (), s32[]{:S(2)}) async-start(), calls=%async_computation.12 | async-start | bytes 1769472 | tf_op jit(solution)/shard_map/all_gather | solution.py:61
  7.9 96.4 %all-gather.11.cloned.1.call-start = ((), (), s32[]{:S(2)}) async-start(), calls=%async_computation.11 | async-start | bytes 3932160 | tf_op jit(solution)/shard_map/all_gather | solution.py:72
  11.7 316.4 %all-gather.15.cloned.1.call-start = ((), (), s32[]{:S(2)}) async-start(), calls=%async_computation.13 | async-start | bytes 1769472 | tf_op jit(solution)/shard_map/all_gather | solution.py:62
  12.4 323.2 %all-gather.17.cloned.1.call-start = ((), (), s32[]{:S(2)}) async-start(), calls=%async_computation.14 | async-start | bytes 1769472 | tf_op jit(solution)/shard_map/all_gather | solution.py:63
  13.0 438.4 %reduce-scatter.14.cloned.1.call-start = ((), (), s32[]{:S(2)}) async-start(), calls=%async_computation.15 | async-start | bytes 7864320 | tf_op jit(solution)/shard_map/reduce_scatter | solution.py:110
  341.9 145.8 %all-gather.21.cloned.1.call-start = ((), (), s32[]{:S(2)}) async-start(), calls=%async_computation.17 | async-start | bytes 3981312 | tf_op jit(solution)/shard_map/all_gather | solution.py:115
  342.5 210.9 %all-gather.19.cloned.1.call-start = ((), (), s32[]{:S(2)}) async-start(), calls=%async_computation.16 | async-start | bytes 3932160 | tf_op jit(solution)/shard_map/all_gather | solution.py:121
  454.2 486.4 %copy-start.48 = (f32[256]{0:T(256)}, f32[256]{0:T(256)S(1)}, u32[]{:S(2)}) copy-start(f32[256]{0:T(256)S(1)} %add_rsqrt_fusion) | copy-start | bytes 3076
  456.5 131.5 %all-gather.23.cloned.1.call-start = ((), (), s32[]{:S(2)}) async-start(), calls=%async_computation.18 | async-start | bytes 3981312 | tf_op jit(solution)/shard_map/all_gather | solution.py:116
  457.2 195.8 %all-gather.27.cloned.1.call-start = ((), (), s32[]{:S(2)}) async-start(), calls=%async_computation.21 | async-start | bytes 3932160 | tf_op jit(solution)/shard_map/all_gather | solution.py:139
  457.9 229.5 %all-gather.25.cloned.1.call-start = ((), (), s32[]{:S(2)}) async-start(), calls=%async_computation.19 | async-start | bytes 3981312 | tf_op jit(solution)/shard_map/all_gather | solution.py:117
  458.5 363.5 %reduce-scatter.18.cloned.1.call-start = ((), (), s32[]{:S(2)}) async-start(), calls=%async_computation.22 | async-start | bytes 7864320 | tf_op jit(solution)/shard_map/reduce_scatter | solution.py:150
  711.1 224.4 %reduce-scatter.16.cloned.1.call-start = ((), (), s32[]{:S(2)}) async-start(), calls=%async_computation.20 | async-start | bytes 7864320 | tf_op jit(solution)/shard_map/reduce_scatter | solution.py:125
  720.7 285.6 %all-gather.29.cloned.1.call-start = ((), (), s32[]{:S(2)}) async-start(), calls=%async_computation.23 | async-start | bytes 3932160 | tf_op jit(solution)/shard_map/all_gather | solution.py:159
  942.1 460.4 %all-reduce.47.cloned.1.call-start = ((), (), s32[]{:S(2)}) async-start(), calls=%async_computation.27 | async-start | bytes 131072 | tf_op jit(solution)/shard_map/psum | solution.py:228
  1286.2 230.1 %reduce-scatter.20.cloned.1.call-start = ((), (), s32[]{:S(2)}) async-start(), calls=%async_computation.24 | async-start | bytes 7864320 | tf_op jit(solution)/shard_map/reduce_scatter | solution.py:210
  1299.3 287.6 %reduce-scatter.30.cloned.1.call-start = ((), (), s32[]{:S(2)}) async-start(), calls=%async_computation.30 | async-start | bytes 7962624 | tf_op jit(solution)/shard_map/reduce_scatter | solution.py:239
  1309.2 347.5 %reduce-scatter.32.cloned.1.call-start = ((), (), s32[]{:S(2)}) async-start(), calls=%async_computation.31 | async-start | bytes 7962624 | tf_op jit(solution)/shard_map/reduce_scatter | solution.py:240
  1319.2 407.1 %reduce-scatter.34.cloned.1.call-start = ((), (), s32[]{:S(2)}) async-start(), calls=%async_computation.32 | async-start | bytes 7962624
  1336.9 427.4 %reduce-scatter.26.cloned.1.call-start = ((), (), s32[]{:S(2)}) async-start(), calls=%async_computation.28 | async-start | bytes 589824 | tf_op jit(solution)/shard_map/reduce_scatter | solution.py:238
  1339.9 474.5 %reduce-scatter.22.cloned.1.call-start = ((), (), s32[]{:S(2)}) async-start(), calls=%async_computation.25 | async-start | bytes 3538944 | tf_op jit(solution)/shard_map/reduce_scatter | solution.py:235
  1345.3 519.7 %reduce-scatter.28.cloned.1.call-start = ((), (), s32[]{:S(2)}) async-start(), calls=%async_computation.29 | async-start | bytes 3538944 | tf_op jit(solution)/shard_map/reduce_scatter | solution.py:237
  1351.9 563.3 %reduce-scatter.24.cloned.1.call-start = ((), (), s32[]{:S(2)}) async-start(), calls=%async_computation.26 | async-start | bytes 3538944 | tf_op jit(solution)/shard_map/reduce_scatter | solution.py:236
  1358.5 202.0 %copy-start.3 = (f32[256,1536]{1,0:T(8,128)S(1)}, f32[256,1536]{1,0:T(8,128)}, u32[]{:S(2)}) copy-start(f32[256,1536]{1,0:T(8,128)} %copy-done.1) | copy-start | bytes 4718596
  (91 other events, 2617.8 us)
Sparse Core Ops, SparseCore 0:
  9.9 28.7 all-gather.12
  40.8 63.4 all-gather.10
  106.3 24.3 all-gather.14
  132.4 25.6 all-gather.16
  342.0 109.3 reduce-scatter.13
  453.2 34.4 all-gather.20
  489.9 63.4 all-gather.18
  555.3 32.6 all-gather.22
  589.5 63.4 all-gather.26
  654.8 32.6 all-gather.24
  711.2 110.7 reduce-scatter.17
  824.2 111.2 reduce-scatter.15
  942.3 64.0 all-gather.28
  1286.3 116.1 all-reduce.46
  1404.7 111.5 reduce-scatter.19
  1520.2 66.5 reduce-scatter.29
  1591.2 65.4 reduce-scatter.31
  1660.7 65.4 reduce-scatter.33
  1730.2 34.1 reduce-scatter.25
  1768.1 46.2 reduce-scatter.21
  1818.7 46.2 reduce-scatter.27
  1868.9 46.2 reduce-scatter.23
where the time goes:
time: 1950 us; the launch traced here: 1920 us
  waiting for transfers between devices  1120 us (57%)
  local copies, waits for them, and re-layouts  442 us (23%)
  other arithmetic  150 us (8%)
  matrix products  138 us (7%)
  blocking collectives  52.4 us (3%)
    slice x63, local copies, waits for them, and re-layouts, local(): lax.associative_scan(combine, (next_decay, d_states.reshape(seq_count, SE...  156 us
    slice x60, local copies, waits for them, and re-layouts, local(): lax.associative_scan(combine, (seq_decay, inflow.reshape(seq_count, SEQ_L...  127 us
    reduce_scatter x1, waiting for transfers between devices, local(): lax.psum_scatter(back_product(hidden, mlp_d), 'tensor', scatter_dimension...  113 us
    reduce_scatter x1, waiting for transfers between devices, local(): lax.psum_scatter(back_product(d_x_low, rec_x) + back_product(d_y_low, rec...  109 us
    reduce_scatter x1, waiting for transfers between devices, local(): lax.psum_scatter(back_product(mixed_out, rec_o), 'tensor', scatter_dimens...  109 us
    reduce_scatter x1, waiting for transfers between devices, local(): lax.psum_scatter(back_product(d_gate_low, mlp_g) + back_product(d_up_low,...  101 us
    unnamed x23, waiting for transfers between devices  74 us
    reduce_scatter x1, waiting for transfers between devices, local(): lax.psum_scatter(mlp_summed[1], 'dp', scatter_dimension=0, tiled=True)  69.9 us
  transfers between devices with their start and end apart: 22, of which 20 were waited for; matrix products, arithmetic and copies ran while one was open for 21% of the time, Pallas kernels for 0%

commit v1 on v0

--- a/solution.py
+++ b/solution.py
@@ -136,7 +136,14 @@
         ]
     )
     upstream = cotangent.astype(jnp.float32)
-    full_cot = lax.all_gather(cotangent, "tensor", axis=0, tiled=True)
+    ring = [cotangent]
+    for hop in range(3):
+        ring.append(lax.ppermute(ring[-1], "tensor", [(dev, (dev + 1) % 4) for dev in range(4)]))
+    full_cot = jnp.roll(
+        jnp.concatenate(ring[::-1], axis=0),
+        (lax.axis_index("tensor") + 1) * ring[0].shape[0],
+        axis=0,
+    )
     d_hidden = jnp.dot(full_cot, mlp_d, preferred_element_type=jnp.float32)
     grad_down = row_product(full_cot, hidden)
     _, pull_mlp = jax.vjp(

time: 1950 us -> 1890 us (0.969)
  waiting for transfers between devices: 1120 us -> 1070 us
    ppermute x0 -> x3, waiting for transfers between devices: none -> 78.5 us  [local(): lax.ppermute(ring[-1], 'tensor', [(dev, (dev + 1) % 4) for dev in range(4)])]
    unnamed x23 -> x21, waiting for transfers between devices: 74 us -> 4.03 us
    reduce_scatter x0 -> x1, waiting for transfers between devices: none -> 69.5 us  [local(): lax.psum_scatter(mlp_summed[2], 'dp', scatter_dimension=0, tiled=True)]
    all_gather x1 -> x0, waiting for transfers between devices: 55.7 us -> none  [local(): full_cot = lax.all_gather(cotangent, 'tensor', axis=0, tiled=True)]
    all_gather x1, waiting for transfers between devices: 65.7 us -> 18.9 us  [local(): full_two = lax.all_gather(n_two, 'tensor', axis=0, tiled=True)]
    all_gather x1, waiting for transfers between devices: 29.1 us -> 0.01 us  [local(): lax.all_gather(w_gate, 'dp', axis=0, tiled=True)]
  transfers between devices with their start and end apart: 22 -> 24, of which waited for: 20 -> 21; matrix products, arithmetic and copies ran while one was open for 21% -> 22% of each run, Pallas kernels for 0% -> 0%
where the time goes in v1:
time: 1890 us; the launch traced here: 1860 us
  waiting for transfers between devices  1070 us (57%)
  local copies, waits for them, and re-layouts  437 us (23%)
  other arithmetic  148 us (8%)
  matrix products  138 us (7%)
  blocking collectives  52.6 us (3%)
    slice x63, local copies, waits for them, and re-layouts, local(): lax.associative_scan(combine, (next_decay, d_states.reshape(seq_count, SE...  152 us
    slice x60, local copies, waits for them, and re-layouts, local(): lax.associative_scan(combine, (seq_decay, inflow.reshape(seq_count, SEQ_L...  123 us
    reduce_scatter x1, waiting for transfers between devices, local(): lax.psum_scatter(back_product(hidden, mlp_d), 'tensor', scatter_dimension...  114 us
    reduce_scatter x1, waiting for transfers between devices, local(): lax.psum_scatter(back_product(d_x_low, rec_x) + back_product(d_y_low, rec...  109 us
    reduce_scatter x1, waiting for transfers between devices, local(): lax.psum_scatter(back_product(mixed_out, rec_o), 'tensor', scatter_dimens...  109 us
    reduce_scatter x1, waiting for transfers between devices, local(): lax.psum_scatter(back_product(d_gate_low, mlp_g) + back_product(d_up_low,...  101 us
    ppermute x3, waiting for transfers between devices, local(): lax.ppermute(ring[-1], 'tensor', [(dev, (dev + 1) % 4) for dev in range(4)])  78.5 us
    reduce_scatter x1, waiting for transfers between devices, local(): lax.psum_scatter(mlp_summed[1], 'dp', scatter_dimension=0, tiled=True)  69.9 us
  transfers between devices with their start and end apart: 24, of which 21 were waited for; matrix products, arithmetic and copies ran while one was open for 22% of the time, Pallas kernels for 0%

profile of v1, /device:TPU:0, one launch (start us, length us, event | category | flops | bytes accessed | tf_op | source)
XLA Modules:
  0.0 1864.4 jit_solution(3670755815463203147)
XLA Ops:
  25.6 13.1 all-gather.12.cloned.1.call-done
  38.7 65.7 %all-gather.10.cloned.1.call-done = bf16[1024,1536]{1,0:T(8,128)(2,1)} async-done(((bf16[256,1536]{1,0:T(8,128)(2,1)}), bf16[1024,1536]{1,0:T(8,128)(2,1)}) %all-gather.10.cloned.1.call-update) | async-done | bytes 3145744 | tf_op jit(solution)/shard_map/all_gather | solution.py:72
  336.8 108.9 %reduce-scatter.12.cloned.1.call-done = f32[256,1536]{1,0:T(8,128)} async-done(((f32[1024,1536]{1,0:T(8,128)}), f32[256,1536]{1,0:T(8,128)}) %reduce-scatter.12.cloned.1.call-update) | async-done | bytes 1572880 | tf_op jit(solution)/shard_map/reduce_scatter | solution.py:110
  453.8 19.8 %collective-permute-done = bf16[256,1536]{1,0:T(8,128)(2,1)S(1)} collective-permute-done((bf16[256,1536]{1,0:T(8,128)(2,1)}, bf16[256,1536]{1,0:T(8,128)(2,1)S(1)}, u32[]{:S(2)}, u32[]{:S(2)}) %collective-permute-start) | collective-permute-done | bytes 786464 | tf_op jit(solution)/shard_map/ppermute | solution.py:141
  474.6 20.4 %collective-permute-done.1 = bf16[256,1536]{1,0:T(8,128)(2,1)} collective-permute-done((bf16[256,1536]{1,0:T(8,128)(2,1)S(1)}, bf16[256,1536]{1,0:T(8,128)(2,1)}, u32[]{:S(2)}, u32[]{:S(2)}) %collective-permute-start.1) | collective-permute-done | bytes 786464 | tf_op jit(solution)/shard_map/ppermute | solution.py:141
  494.9 38.3 %collective-permute-done.2 = bf16[256,1536]{1,0:T(8,128)(2,1)} collective-permute-done((bf16[256,1536]{1,0:T(8,128)(2,1)}, bf16[256,1536]{1,0:T(8,128)(2,1)}, u32[]{:S(2)}, u32[]{:S(2)}) %collective-permute-start.2) | collective-permute-done | bytes 786464 | tf_op jit(solution)/shard_map/ppermute | solution.py:141
  545.4 18.9 %all-gather.18.cloned.1.call-done = bf16[1024,1536]{1,0:T(8,128)(2,1)} async-done(((bf16[256,1536]{1,0:T(8,128)(2,1)}), bf16[1024,1536]{1,0:T(8,128)(2,1)}) %all-gather.18.cloned.1.call-update) | async-done | bytes 3145744 | tf_op jit(solution)/shard_map/all_gather | solution.py:121
  573.8 25.2 %all-gather.22.cloned.1.call-done = bf16[1536,1152]{1,0:T(8,128)(2,1)} async-done(((bf16[192,1152]{1,0:T(8,128)(2,1)}), bf16[1536,1152]{1,0:T(8,128)(2,1)}) %all-gather.22.cloned.1.call-update) | async-done | bytes 3538960 | tf_op jit(solution)/shard_map/all_gather | solution.py:116
  608.3 26.6 %all-gather.24.cloned.1.call-done = bf16[1536,1152]{1,0:T(8,128)(2,1)} async-done(((bf16[192,1152]{1,0:T(8,128)(2,1)}), bf16[1536,1152]{1,0:T(8,128)(2,1)}) %all-gather.24.cloned.1.call-update) | async-done | bytes 3538960 | tf_op jit(solution)/shard_map/all_gather | solution.py:117
  634.8 13.0 multiply_convert_fusion
  668.2 101.1 %reduce-scatter.16.cloned.1.call-done = f32[256,1536]{1,0:T(8,128)} async-done(((f32[1024,1536]{1,0:T(8,128)}), f32[256,1536]{1,0:T(8,128)}) %reduce-scatter.16.cloned.1.call-update) | async-done | bytes 1572880 | tf_op jit(solution)/shard_map/reduce_scatter | solution.py:157
  769.3 113.6 %reduce-scatter.14.cloned.1.call-done = f32[256,1536]{1,0:T(8,128)} async-done(((f32[1024,1536]{1,0:T(8,128)}), f32[256,1536]{1,0:T(8,128)}) %reduce-scatter.14.cloned.1.call-update) | async-done | bytes 1572880 | tf_op jit(solution)/shard_map/reduce_scatter | solution.py:125
  962.8 16.7 reverse.6
  1163.9 16.7 rev.8
  1297.0 47.7 %all-reduce.47.cloned.1.call-done = f32[8,2048]{1,0:T(8,128)} async-done(((f32[8,2048]{1,0:T(8,128)}), f32[8,2048]{1,0:T(8,128)}) %all-reduce.47.cloned.1.call-update) | async-done | bytes 65552 | tf_op jit(solution)/shard_map/psum | solution.py:235
  1349.1 109.3 %reduce-scatter.18.cloned.1.call-done = f32[256,1536]{1,0:T(8,128)} async-done(((f32[1024,1536]{1,0:T(8,128)}), f32[256,1536]{1,0:T(8,128)}) %reduce-scatter.18.cloned.1.call-update) | async-done | bytes 1572880 | tf_op jit(solution)/shard_map/reduce_scatter | solution.py:217
  1460.3 41.2 %all-reduce.44 = (f32[2,1536]{1,0:T(2,128)S(1)}, f32[4]{0:T(128)S(1)}) all-reduce(f32[2,1536]{1,0:T(2,128)S(1)} %pad_maximum_fusion.15, f32[4]{0:T(128)S(1)} %pad_maximum_fusion.20), channel_id=1, replica_groups=mesh['dp'=8,'tensor'=4] {'dp','tensor'}, use_global_device_ids=true, to_apply=%region_10.11 | all-reduce | flops 3076 | bytes 24608 | tf_op jit(solution)/shard_map/psum | solution.py:235
  1506.5 22.5 %reduce-scatter.28.cloned.1.call-done = f32[192,1152]{1,0:T(8,128)} async-done(((f32[1536,1152]{1,0:T(8,128)}), f32[192,1152]{1,0:T(8,128)}) %reduce-scatter.28.cloned.1.call-update) | async-done | bytes 884752 | tf_op jit(solution)/shard_map/reduce_scatter | solution.py:246
  1529.0 69.9 %reduce-scatter.30.cloned.1.call-done = f32[192,1152]{1,0:T(8,128)} async-done(((f32[1536,1152]{1,0:T(8,128)}), f32[192,1152]{1,0:T(8,128)}) %reduce-scatter.30.cloned.1.call-update) | async-done | bytes 884752 | tf_op jit(solution)/shard_map/reduce_scatter | solution.py:247
  1598.9 69.5 %reduce-scatter.32.cloned.1.call-done = f32[192,1152]{1,0:T(8,128)} async-done(((f32[1536,1152]{1,0:T(8,128)}), f32[192,1152]{1,0:T(8,128)}) %reduce-scatter.32.cloned.1.call-update) | async-done | bytes 884752 | tf_op jit(solution)/shard_map/reduce_scatter | solution.py:248
  1668.4 37.9 %reduce-scatter.24.cloned.1.call-done = f32[2,4,16,128]{3,2,1,0:T(8,128)} async-done(((f32[2,4,128,128]{3,2,1,0:T(8,128)}), f32[2,4,16,128]{3,2,1,0:T(8,128)}) %reduce-scatter.24.cloned.1.call-update) | async-done | bytes 65552 | tf_op jit(solution)/shard_map/reduce_scatter | solution.py:245
  1706.3 50.2 %reduce-scatter.20.cloned.1.call-done = f32[192,512]{1,0:T(8,128)} async-done(((f32[1536,512]{1,0:T(8,128)}), f32[192,512]{1,0:T(8,128)}) %reduce-scatter.20.cloned.1.call-update) | async-done | bytes 393232 | tf_op jit(solution)/shard_map/reduce_scatter | solution.py:242
  1756.5 50.5 %reduce-scatter.26.cloned.1.call-done = f32[192,512]{1,0:T(8,128)} async-done(((f32[1536,512]{1,0:T(8,128)}), f32[192,512]{1,0:T(8,128)}) %reduce-scatter.26.cloned.1.call-update) | async-done | bytes 393232 | tf_op jit(solution)/shard_map/reduce_scatter | solution.py:244
  1807.0 50.2 %reduce-scatter.22.cloned.1.call-done = f32[192,512]{1,0:T(8,128)} async-done(((f32[1536,512]{1,0:T(8,128)}), f32[192,512]{1,0:T(8,128)}) %reduce-scatter.22.cloned.1.call-update) | async-done | bytes 393232 | tf_op jit(solution)/shard_map/reduce_scatter | solution.py:243
  (567 shorter events, 701.4 us)
Async XLA Ops:
  7.2 31.5 %all-gather.12.cloned.1.call-start = ((), (), s32[]{:S(2)}) async-start(), calls=%async_computation.12 | async-start | bytes 1769472 | tf_op jit(solution)/shard_map/all_gather | solution.py:61
  7.9 96.4 %all-gather.10.cloned.1.call-start = ((), (), s32[]{:S(2)}) async-start(), calls=%async_computation.11 | async-start | bytes 3932160 | tf_op jit(solution)/shard_map/all_gather | solution.py:72
  11.7 310.8 %all-gather.14.cloned.1.call-start = ((), (), s32[]{:S(2)}) async-start(), calls=%async_computation.13 | async-start | bytes 1769472 | tf_op jit(solution)/shard_map/all_gather | solution.py:62
  12.4 317.5 %all-gather.16.cloned.1.call-start = ((), (), s32[]{:S(2)}) async-start(), calls=%async_computation.14 | async-start | bytes 1769472 | tf_op jit(solution)/shard_map/all_gather | solution.py:63
  13.0 432.8 %reduce-scatter.12.cloned.1.call-start = ((), (), s32[]{:S(2)}) async-start(), calls=%async_computation.15 | async-start | bytes 7864320 | tf_op jit(solution)/shard_map/reduce_scatter | solution.py:110
  336.2 209.2 %all-gather.20.cloned.1.call-start = ((), (), s32[]{:S(2)}) async-start(), calls=%async_computation.17 | async-start | bytes 3981312 | tf_op jit(solution)/shard_map/all_gather | solution.py:115
  336.8 227.6 %all-gather.18.cloned.1.call-start = ((), (), s32[]{:S(2)}) async-start(), calls=%async_computation.16 | async-start | bytes 3932160 | tf_op jit(solution)/shard_map/all_gather | solution.py:121
  450.8 148.2 %all-gather.22.cloned.1.call-start = ((), (), s32[]{:S(2)}) async-start(), calls=%async_computation.18 | async-start | bytes 3981312 | tf_op jit(solution)/shard_map/all_gather | solution.py:116
  451.5 183.3 %all-gather.24.cloned.1.call-start = ((), (), s32[]{:S(2)}) async-start(), calls=%async_computation.19 | async-start | bytes 3981312 | tf_op jit(solution)/shard_map/all_gather | solution.py:117
  452.3 317.0 %reduce-scatter.16.cloned.1.call-start = ((), (), s32[]{:S(2)}) async-start(), calls=%async_computation.21 | async-start | bytes 7864320 | tf_op jit(solution)/shard_map/reduce_scatter | solution.py:157
  452.3 21.4 %collective-permute-start = (bf16[256,1536]{1,0:T(8,128)(2,1)}, bf16[256,1536]{1,0:T(8,128)(2,1)S(1)}, u32[]{:S(2)}, u32[]{:S(2)}) collective-permute-start(bf16[256,1536]{1,0:T(8,128)(2,1)} %param.29), channel_id=1, source_target_pairs={{0,1},{1,2},{2,3},{3,0},{4,5},{5,6},{6,7},{7,4},{8,9},{9,10},{10,1... | collective-permute-start | bytes 2359304 | tf_op jit(solution)/shard_map/ppermute | solution.py:141
  474.6 20.4 %collective-permute-start.1 = (bf16[256,1536]{1,0:T(8,128)(2,1)S(1)}, bf16[256,1536]{1,0:T(8,128)(2,1)}, u32[]{:S(2)}, u32[]{:S(2)}) collective-permute-start(bf16[256,1536]{1,0:T(8,128)(2,1)S(1)} %collective-permute-done), channel_id=1, source_target_pairs={{0,1},{1,2},{2,3},{3,0},{4,5},{5,6},{6,7},{7,4},{8,9},{9,10},{10,1... | collective-permute-start | bytes 2359304 | tf_op jit(solution)/shard_map/ppermute | solution.py:141
  494.9 38.3 %collective-permute-start.2 = (bf16[256,1536]{1,0:T(8,128)(2,1)}, bf16[256,1536]{1,0:T(8,128)(2,1)}, u32[]{:S(2)}, u32[]{:S(2)}) collective-permute-start(bf16[256,1536]{1,0:T(8,128)(2,1)} %collective-permute-done.1), channel_id=1, source_target_pairs={{0,1},{1,2},{2,3},{3,0},{4,5},{5,6},{6,7},{7,4},{8,9},{9,10},{10,1... | collective-permute-start | bytes 2359304 | tf_op jit(solution)/shard_map/ppermute | solution.py:141
  658.4 224.5 %reduce-scatter.14.cloned.1.call-start = ((), (), s32[]{:S(2)}) async-start(), calls=%async_computation.20 | async-start | bytes 7864320 | tf_op jit(solution)/shard_map/reduce_scatter | solution.py:125
  668.1 285.7 %all-gather.26.cloned.1.call-start = ((), (), s32[]{:S(2)}) async-start(), calls=%async_computation.22 | async-start | bytes 3932160 | tf_op jit(solution)/shard_map/all_gather | solution.py:166
  889.6 455.1 %all-reduce.47.cloned.1.call-start = ((), (), s32[]{:S(2)}) async-start(), calls=%async_computation.26 | async-start | bytes 131072 | tf_op jit(solution)/shard_map/psum | solution.py:235
  1228.4 230.1 %reduce-scatter.18.cloned.1.call-start = ((), (), s32[]{:S(2)}) async-start(), calls=%async_computation.23 | async-start | bytes 7864320 | tf_op jit(solution)/shard_map/reduce_scatter | solution.py:217
  1242.0 287.1 %reduce-scatter.28.cloned.1.call-start = ((), (), s32[]{:S(2)}) async-start(), calls=%async_computation.29 | async-start | bytes 7962624 | tf_op jit(solution)/shard_map/reduce_scatter | solution.py:246
  1251.9 347.0 %reduce-scatter.30.cloned.1.call-start = ((), (), s32[]{:S(2)}) async-start(), calls=%async_computation.30 | async-start | bytes 7962624 | tf_op jit(solution)/shard_map/reduce_scatter | solution.py:247
  1261.8 406.6 %reduce-scatter.32.cloned.1.call-start = ((), (), s32[]{:S(2)}) async-start(), calls=%async_computation.31 | async-start | bytes 7962624 | tf_op jit(solution)/shard_map/reduce_scatter | solution.py:248
  1271.8 434.5 %reduce-scatter.24.cloned.1.call-start = ((), (), s32[]{:S(2)}) async-start(), calls=%async_computation.27 | async-start | bytes 589824 | tf_op jit(solution)/shard_map/reduce_scatter | solution.py:245
  1274.8 481.7 %reduce-scatter.20.cloned.1.call-start = ((), (), s32[]{:S(2)}) async-start(), calls=%async_computation.24 | async-start | bytes 3538944 | tf_op jit(solution)/shard_map/reduce_scatter | solution.py:242
  1280.3 526.7 %reduce-scatter.26.cloned.1.call-start = ((), (), s32[]{:S(2)}) async-start(), calls=%async_computation.28 | async-start | bytes 3538944 | tf_op jit(solution)/shard_map/reduce_scatter | solution.py:244
  1286.9 570.3 %reduce-scatter.22.cloned.1.call-start = ((), (), s32[]{:S(2)}) async-start(), calls=%async_computation.25 | async-start | bytes 3538944 | tf_op jit(solution)/shard_map/reduce_scatter | solution.py:243
  (98 other events, 3586.9 us)
Sparse Core Ops, SparseCore 0:
  9.9 28.7 all-gather.11
  40.8 63.4 all-gather.9
  106.3 24.3 all-gather.13
  132.4 25.6 all-gather.15
  336.3 109.4 reduce-scatter.11
  447.5 34.4 all-gather.19
  484.2 80.1 all-gather.17
  566.2 32.6 all-gather.21
  600.8 33.9 all-gather.23
  658.5 110.7 reduce-scatter.15
  771.6 111.2 reduce-scatter.13
  889.7 64.0 all-gather.25
  1228.5 116.1 all-reduce.46
  1346.9 111.5 reduce-scatter.17
  1462.4 66.5 reduce-scatter.27
  1533.4 65.4 reduce-scatter.29
  1602.8 65.4 reduce-scatter.31
  1672.2 34.0 reduce-scatter.23
  1710.2 46.2 reduce-scatter.19
  1760.7 46.2 reduce-scatter.25
  1810.9 46.2 reduce-scatter.21
